TPU v7x, 128 devices: a whole 4x4x4 slice. The times are simulated.
128 devices in a mesh: gx: 16 (over x, z_lo, core), gy: 8 (over z_hi, y).
Axes of the slice: x: 4, y: 4, z: 4 (z_hi: 2, z_lo: 2; z = z_hi * 2 + z_lo), core: 2. Of those that a mesh axis runs over, the one named last changes fastest.
Arguments:
- fields: float32 [5, 256, 256, 128], P(None, 'gx', 'gy'), may hold values from -6 to 6
- patch_weight: bfloat16 [2560, 512], replicated, may hold values from -0.125 to 0.125
- trainer_of: int32 [8192, 1], P(('gx', 'gy')), may hold values from 0 to 127; in each aligned block of 64 rows (0 to 63, 64 to 127, ...) at most 2 rows name the same one
- lag_index: int32 [32, 32, 16], P('gx', 'gy'), may hold values from 0 to 1
- w_in: bfloat16 [128, 512, 2048], P(('gx', 'gy')), may hold values from -0.25 to 0.25
- b_in: float32 [128, 2048], P(('gx', 'gy')), may hold values from -3 to 3
- w_out: bfloat16 [128, 2048, 512], P(('gx', 'gy')), may hold values from -0.125 to 0.125
- b_out: float32 [128, 512], P(('gx', 'gy')), may hold values from -3 to 3
Outputs:
- new_fields: float32 [5, 256, 256, 128], P(None, 'gx', 'gy')
- patch_gradient: float32 [2560, 512], replicated
- w_in_gradient: float32 [128, 512, 2048], P(('gx', 'gy'))
- b_in_gradient: float32 [128, 2048], P(('gx', 'gy'))
- w_out_gradient: float32 [128, 2048, 512], P(('gx', 'gy'))
- b_out_gradient: float32 [128, 512], P(('gx', 'gy'))
Inputs may be any that keep to these rules, and one draw needn't show every extreme that they name: `trainer_of`: among the 64 rows of one brick, no trainer is named more than 2 times.
All inputs are finite; a program needn't handle non-finite values.
Results may differ from a plain program's by a relative error of at most 0.0062.
Values may be sent and summed in bfloat16 or wider, within the bound.
No kernel may reach another device: no remote copies, remote signals or barrier semaphores. Data moves between devices by JAX's collectives and lax.ppermute only.
A program may use at most 128 MiB of HBM per device.

v0:
```python
import jax
import jax.numpy as jnp
from jax import lax
from jax.sharding import PartitionSpec as P

FIELDS = 5
PATCH = 8
STEPS = 3
EMBED = 512
BLOCK_ROWS = 2
time_step = 0.2
viscosity = 0.5
drift_x = 0.6
drift_y = -0.4
drift_z = 0.3
error_weight = 0.0625


def with_halo(x, sides, width):
    edges = {}
    for axis, dim in sides:
        count, length = (lax.axis_size(axis), x.shape[dim])
        up = [(i, (i + 1) % count) for i in range(count - 1)]
        last = lax.slice_in_dim(x, length - width, length, axis=dim)
        initial = lax.slice_in_dim(x, 0, width, axis=dim)
        edges[dim] = (
            lax.ppermute(last, axis, up),
            lax.ppermute(initial, axis, [(b, a) for a, b in up]),
        )
    done = []
    for _, dim in sides:
        low, high = edges[dim]
        around = [(width, width) if d in done else (0, 0) for d in range(x.ndim)]
        x = jnp.concatenate([jnp.pad(low, around), x, jnp.pad(high, around)], axis=dim)
        done.append(dim)
    return x


def sent_together(arrays, axis, split_dim, concat_dim, along):
    columns = [a.reshape(*a.shape[:along], -1) for a in arrays]
    both = jnp.concatenate(columns, axis=along)
    result, at, finished = (
        lax.all_to_all(both, axis, split_axis=split_dim, concat_axis=concat_dim, tiled=True),
        0,
        [],
    )
    for a, column in zip(arrays, columns):
        piece = result[..., at : at + column.shape[along]]
        finished.append(piece.reshape(*piece.shape[:along], *a.shape[along:]))
        at += column.shape[along]
    return tuple(finished)


def shifted(padded, dimension, offset):
    window = [slice(None)]
    for other in (1, 2, 3):
        window.append(slice(2, padded.shape[other] - 2))
    window[dimension] = slice(2 + offset, padded.shape[dimension] - 2 + offset)
    return padded[tuple(window)]


def tendency(padded):
    gradients = []
    laplacian = 0.0
    for dimension in (1, 2, 3):
        back_two = shifted(padded, dimension, -2)
        back_one = shifted(padded, dimension, -1)
        middle = shifted(padded, dimension, 0)
        ahead_one = shifted(padded, dimension, 1)
        ahead_two = shifted(padded, dimension, 2)
        gradients.append((back_two - 8.0 * back_one + 8.0 * ahead_one - ahead_two) / 12.0)
        laplacian = (
            laplacian
            + (-back_two + 16.0 * back_one - 30.0 * middle + 16.0 * ahead_one - ahead_two) / 12.0
        )
    carried = drift_x * gradients[0] + drift_y * gradients[1] + drift_z * gradients[2]
    divergence = gradients[0][1] + gradients[1][2] + gradients[2][3]
    acoustic = jnp.stack(
        [divergence, gradients[0][4], gradients[1][4], gradients[2][4], divergence]
    )
    return viscosity * laplacian - carried - acoustic


def contract_rows(left, right):
    return lax.dot_general(
        left, right, (((0,), (0,)), ((), ())), preferred_element_type=jnp.float32
    )


def contract_cols(left, right):
    return lax.dot_general(
        left, right, (((1,), (1,)), ((), ())), preferred_element_type=jnp.float32
    )


def trainer_step(source, target, valid, w_first, b_first, w_second, b_second):
    pre = jnp.dot(source, w_first, preferred_element_type=jnp.float32) + b_first
    hidden = jax.nn.silu(pre).astype(jnp.bfloat16)
    predict = jnp.dot(hidden, w_second, preferred_element_type=jnp.float32) + b_second
    error = (error_weight * (predict - target.astype(jnp.float32)) * valid).astype(jnp.bfloat16)
    b_second_grad = jnp.sum(error.astype(jnp.float32), axis=0)
    w_second_grad = contract_rows(hidden, error)
    back = contract_cols(error, w_second)
    sigma = jax.nn.sigmoid(pre)
    pre_grad = (back * sigma * (1.0 + pre * (1.0 - sigma))).astype(jnp.bfloat16)
    b_first_grad = jnp.sum(pre_grad.astype(jnp.float32), axis=0)
    w_first_grad = contract_rows(source, pre_grad)
    source_grad = contract_cols(pre_grad, w_first).astype(jnp.bfloat16)
    return (source_grad, w_first_grad, b_first_grad, w_second_grad, b_second_grad)


def patchify(state):
    width_x, width_y, width_z = (state.shape[1], state.shape[2], state.shape[3])
    shaped = state.reshape(
        FIELDS, width_x // PATCH, PATCH, width_y // PATCH, PATCH, width_z // PATCH, PATCH
    )
    return shaped.transpose(1, 3, 5, 0, 2, 4, 6).reshape(-1, FIELDS * PATCH**3)


def pad_third(current):
    return jnp.pad(current, ((0, 0), (0, 0), (0, 0), (2, 2)))


def advance(fields):
    states = []
    current = fields
    for counter in range(STEPS):
        padded = with_halo(current, (("gx", 1), ("gy", 2)), 2)
        current = current + time_step * tendency(pad_third(padded))
        states.append(current)
    return states


def per_device(fields, patch_weight, trainer_of, lag_index, w_in, b_in, w_out, b_out):
    states = advance(fields)
    devices = lax.axis_size("gx") * lax.axis_size("gy")
    lag_rows = lag_index.reshape(-1, 1)
    picked = patchify(states[0].astype(jnp.bfloat16))
    picked = jnp.where(lag_rows == 1, patchify(states[1].astype(jnp.bfloat16)), picked)
    target = jnp.dot(
        patchify(states[-1].astype(jnp.bfloat16)), patch_weight, preferred_element_type=jnp.float32
    ).astype(jnp.bfloat16)
    patch_count = picked.shape[0]
    block_count = patch_count // BLOCK_ROWS
    slot_count = max(2, 2 * block_count // devices)
    owners = trainer_of[:, 0]
    onehot = (owners[:, None] == jnp.arange(devices, dtype=jnp.int32)[None, :]).astype(jnp.int32)
    within_rank = jnp.sum((jnp.cumsum(onehot, axis=0) - onehot) * onehot, axis=1)
    block_slot = owners * slot_count + within_rank

    def into_slots(rows):
        width = rows.shape[1]
        blocks = rows.reshape(block_count, BLOCK_ROWS, width)
        buffer = (
            jnp.zeros((devices * slot_count, BLOCK_ROWS, width), rows.dtype)
            .at[block_slot]
            .set(blocks)
        )
        return buffer.reshape(devices, slot_count, BLOCK_ROWS, width)

    valid_send = jnp.zeros((devices * slot_count,), jnp.bfloat16).at[block_slot].set(1.0)
    valid_send = valid_send.reshape(devices, slot_count)
    source = jnp.dot(picked, patch_weight, preferred_element_type=jnp.float32).astype(jnp.bfloat16)
    got_source, got_target, got_valid = sent_together(
        (into_slots(source), into_slots(target), valid_send), ("gx", "gy"), 0, 0, 2
    )
    valid_rows = jnp.repeat(got_valid.astype(jnp.float32).reshape(-1), BLOCK_ROWS)[:, None]
    results = trainer_step(
        got_source.reshape(-1, EMBED),
        got_target.reshape(-1, EMBED),
        valid_rows,
        w_in[0],
        b_in[0],
        w_out[0],
        b_out[0],
    )
    returned = lax.all_to_all(
        results[0].reshape(devices, slot_count, BLOCK_ROWS, EMBED),
        ("gx", "gy"),
        split_axis=0,
        concat_axis=0,
        tiled=True,
    )
    source_grad = returned.reshape(devices * slot_count, BLOCK_ROWS, EMBED)[block_slot]
    partial_value = contract_rows(picked, source_grad.reshape(patch_count, EMBED))
    patch_gradient = lax.psum(partial_value, ("gx", "gy"))
    return (
        states[-1],
        patch_gradient,
        results[1][None],
        results[2][None],
        results[3][None],
        results[4][None],
    )


def solution(mesh):
    in_specs = (
        P(None, "gx", "gy", None),
        P(),
        P(("gx", "gy"), None),
        P("gx", "gy", None),
        P(("gx", "gy"), None, None),
        P(("gx", "gy"), None),
        P(("gx", "gy"), None, None),
        P(("gx", "gy"), None),
    )
    out_specs = (
        P(None, "gx", "gy", None),
        P(),
        P(("gx", "gy"), None, None),
        P(("gx", "gy"), None),
        P(("gx", "gy"), None, None),
        P(("gx", "gy"), None),
    )
    return jax.shard_map(
        per_device, mesh=mesh, in_specs=in_specs, out_specs=out_specs, check_vma=False
    )
```

profile of v0, /device:TPU:1, one launch (start us, length us, event | category | flops | bytes accessed | tf_op | source)
XLA Modules:
  0.0 482.5 jit_solution(16049055990114909716)
XLA Ops:
  8.5 4.7 collective-permute-start.2
  38.8 4.9 %collective-permute-start.6 = (f32[5,16,2,128]{3,2,1,0:T(2,128)S(1)}, f32[5,16,2,128]{3,2,1,0:T(2,128)}, u32[]{:S(2)}, u32[]{:S(2)}) collective-permute-start(f32[5,16,2,128]{3,2,1,0:T(2,128)S(1)} %get-tuple-element.34), channel_id=1, source_target_pairs={{0,1},{1,2},{2,3},{3,4},{4,5},{5,6},{6,7},{8,9},{9,10},{10,11},{11... | collective-permute-start | bytes 245768 | tf_op jit(solution)/shard_map/ppermute | solution.py:27
  51.6 14.5 %reshape.74 = bf16[5,2,8,4,8,16,8]{6,5,4,3,2,1,0:T(8,128)(2,1)} reshape(bf16[5,16,32,128]{3,2,1,0:T(8,128)(2,1)} %get-tuple-element.10) | data formatting | bytes 1310720 | tf_op jit(solution)/shard_map/reshape | solution.py:114
  66.1 13.3 %copy.21 = bf16[2,4,16,5,8,8,8]{2,1,0,6,5,4,3:T(4,128)(2,1)} copy(bf16[2,4,16,5,8,8,8]{6,2,5,1,4,0,3:T(8,128)(2,1)} %bitcast.73) | data formatting | bytes 1310720 | tf_op jit(solution)/shard_map/transpose | solution.py:117
  79.4 8.1 %reshape.76 = bf16[128,2560]{0,1:T(8,128)(2,1)} reshape(bf16[2,4,16,5,8,8,8]{2,1,0,6,5,4,3:T(4,128)(2,1)} %copy.21) | data formatting | bytes 1310720 | tf_op jit(solution)/shard_map/reshape | solution.py:117
  89.4 4.6 select_maximum_fusion.4
  102.4 4.9 %collective-permute-start.10 = (f32[5,16,2,128]{3,2,1,0:T(2,128)}, f32[5,16,2,128]{3,2,1,0:T(2,128)}, u32[]{:S(2)}, u32[]{:S(2)}) collective-permute-start(f32[5,16,2,128]{3,2,1,0:T(2,128)} %get-tuple-element.30), channel_id=1, source_target_pairs={{0,1},{1,2},{2,3},{3,4},{4,5},{5,6},{6,7},{8,9},{9,10},{10,11},{11... | collective-permute-start | bytes 245768 | tf_op jit(solution)/shard_map/ppermute | solution.py:27
  114.6 14.4 %reshape.73 = bf16[5,2,8,4,8,16,8]{6,5,4,3,2,1,0:T(8,128)(2,1)} reshape(bf16[5,16,32,128]{3,2,1,0:T(8,128)(2,1)} %get-tuple-element.8) | data formatting | bytes 1310720 | tf_op jit(solution)/shard_map/reshape | solution.py:114
  129.1 13.3 %copy.20 = bf16[2,4,16,5,8,8,8]{2,1,0,6,5,4,3:T(4,128)(2,1)} copy(bf16[2,4,16,5,8,8,8]{6,2,5,1,4,0,3:T(8,128)(2,1)} %bitcast.74) | data formatting | bytes 1310720 | tf_op jit(solution)/shard_map/transpose | solution.py:117
  142.4 8.1 %reshape.75 = bf16[128,2560]{0,1:T(8,128)(2,1)} reshape(bf16[2,4,16,5,8,8,8]{2,1,0,6,5,4,3:T(4,128)(2,1)} %copy.20) | data formatting | bytes 1310720 | tf_op jit(solution)/shard_map/reshape | solution.py:117
  153.3 5.4 %scatter_fusion = bf16[256,2,512]{2,1,0:T(2,128)(2,1)S(1)} fusion(bf16[256,2,512]{2,1,0:T(2,128)(2,1)S(1)} %broadcast.110.clone.1, s32[64]{0:T(128)S(1)} %fusion.50, bf16[64,2,512]{2,1,0:T(2,128)(2,1)} %reshape.97), kind=kCustom, calls=%fused_computation.1 | custom fusion | bytes 393472 | tf_op jit(solution)/shard_map/scatter | solution.py:157
  161.7 4.6 select_maximum_fusion
  173.1 14.4 %reshape.78 = bf16[5,2,8,4,8,16,8]{6,5,4,3,2,1,0:T(8,128)(2,1)} reshape(bf16[5,16,32,128]{3,2,1,0:T(8,128)(2,1)} %get-tuple-element.6) | data formatting | bytes 1310720 | tf_op jit(solution)/shard_map/reshape | solution.py:114
  187.6 13.3 %copy.22 = bf16[2,4,16,5,8,8,8]{2,1,0,6,5,4,3:T(4,128)(2,1)} copy(bf16[2,4,16,5,8,8,8]{6,2,5,1,4,0,3:T(8,128)(2,1)} %bitcast.75) | data formatting | bytes 1310720 | tf_op jit(solution)/shard_map/transpose | solution.py:117
  200.9 7.5 %reshape.79 = bf16[128,2560]{0,1:T(8,128)(2,1)S(1)} reshape(bf16[2,4,16,5,8,8,8]{2,1,0,6,5,4,3:T(4,128)(2,1)} %copy.22) | data formatting | bytes 1310720 | tf_op jit(solution)/shard_map/reshape | solution.py:117
  214.0 20.5 %all-to-all-start = ((bf16[128,2,2049]{2,1,0:T(2,128)(2,1)}), bf16[128,2,2049]{2,1,0:T(2,128)(2,1)S(1)}, u32[]{:S(2)}, u32[]{:S(2)}) async-start(bf16[128,2,2049]{2,1,0:T(2,128)(2,1)} %pad_maximum_fusion.8), calls=%async_computation | async-start | bytes 2228224 | tf_op jit(solution)/shard_map/all_to_all | solution.py:43
  234.5 19.8 %all-to-all-done = bf16[128,2,2049]{2,1,0:T(2,128)(2,1)S(1)} async-done(((bf16[128,2,2049]{2,1,0:T(2,128)(2,1)}), bf16[128,2,2049]{2,1,0:T(2,128)(2,1)S(1)}, u32[]{:S(2)}, u32[]{:S(2)}) %all-to-all-start) | async-done | bytes 1049120 | tf_op jit(solution)/shard_map/all_to_all | solution.py:43
  269.5 5.0 %all-to-all-start.1 = ((bf16[128,2,2,512]{3,2,1,0:T(2,128)(2,1)}), bf16[128,2,2,512]{3,2,1,0:T(2,128)(2,1)S(1)}, u32[]{:S(2)}, u32[]{:S(2)}) async-start(bf16[128,2,2,512]{3,2,1,0:T(2,128)(2,1)} %reshape.81), calls=%async_computation.1 | async-start | bytes 1048576 | tf_op jit(solution)/shard_map/all_to_all | solution.py:177
  274.6 12.3 %broadcast_select_fusion = bf16[2,4,16,5,8,8,8]{6,2,5,1,4,0,3:T(8,128)(2,1)} fusion(pred[2,4,16]{2,1,0:T(4,128)(4,1)S(1)} %broadcast_compare_fusion, bf16[5,2,8,4,8,16,8]{6,5,4,3,2,1,0:T(8,128)(2,1)} %reshape.74, bf16[5,2,8,4,8,16,8]{6,5,4,3,2,1,0:T(8,128)(2,1)} %reshape.73), kind=kLoop, calls=%fused_computation.4 | loop fusion | flops 327680 | bytes 1966208 | tf_op jit(solution)/shard_map/jit(_where)/select_n | solution.py:139
  286.9 13.3 %copy.19 = bf16[2,4,16,5,8,8,8]{2,1,0,6,5,4,3:T(4,128)(2,1)} copy(bf16[2,4,16,5,8,8,8]{6,2,5,1,4,0,3:T(8,128)(2,1)} %broadcast_select_fusion) | data formatting | bytes 1310720 | tf_op jit(solution)/shard_map/jit(_where)/select_n | solution.py:139
  300.2 7.3 %select_n.17 = bf16[128,2560]{0,1:T(8,128)(2,1)S(1)} reshape(bf16[2,4,16,5,8,8,8]{2,1,0,6,5,4,3:T(4,128)(2,1)} %copy.19) | data formatting | bytes 1310720 | tf_op jit(solution)/shard_map/jit(_where)/select_n | solution.py:139
  311.7 5.0 %convolution_bitcast_fusion.1 = f32[1,512,2048]{2,1,0:T(8,128)} fusion(bf16[512,512]{1,0:T(8,128)(2,1)S(1)} %reshape_reshape.16, bf16[512,2048]{1,0:T(8,128)(2,1)} %copy-done.11), kind=kOutput, calls=%fused_computation.23 | convolution fusion | flops 1073741824 | bytes 6815744 | tf_op jit(solution)/shard_map/dot_general | solution.py:85
  320.2 149.4 %all-reduce.11.cloned.1.call-done = f32[2560,512]{1,0:T(8,128)} async-done(((f32[2560,512]{1,0:T(8,128)}), f32[2560,512]{1,0:T(8,128)}) %all-reduce.11.cloned.1.call-update) | async-done | bytes 5242896 | tf_op jit(solution)/shard_map/psum | solution.py:186
  469.6 5.6 %copy.44 = f32[2560,512]{1,0:T(8,128)} copy(f32[2560,512]{1,0:T(8,128)} %all-reduce.11.cloned.1.call-done) | data formatting | bytes 10485760
  (138 shorter events, 92.9 us)
Async XLA Ops:
  7.2 143.3 %copy-start = (bf16[2560,512]{1,0:T(8,128)(2,1)S(1)}, bf16[2560,512]{1,0:T(8,128)(2,1)}, u32[]{:S(2)}) copy-start(bf16[2560,512]{1,0:T(8,128)(2,1)} %param.9) | copy-start | bytes 7864324
  8.5 15.7 %collective-permute-start.2 = (f32[5,16,2,128]{3,2,1,0:T(2,128)S(1)}, f32[5,16,2,128]{3,2,1,0:T(2,128)}, u32[]{:S(2)}, u32[]{:S(2)}) collective-permute-start(f32[5,16,2,128]{3,2,1,0:T(2,128)S(1)} %get-tuple-element.39), channel_id=1, source_target_pairs={{0,1},{1,2},{2,3},{3,4},{4,5},{5,6},{6,7},{8,9},{9,10},{10,11},{11... | collective-permute-start | bytes 245768 | tf_op jit(solution)/shard_map/ppermute | solution.py:27
  13.1 11.9 %collective-permute-start.3 = (f32[5,16,2,128]{3,2,1,0:T(2,128)S(1)}, f32[5,16,2,128]{3,2,1,0:T(2,128)}, u32[]{:S(2)}, u32[]{:S(2)}) collective-permute-start(f32[5,16,2,128]{3,2,1,0:T(2,128)S(1)} %get-tuple-element.40), channel_id=1, source_target_pairs={{1,0},{2,1},{3,2},{4,3},{5,4},{6,5},{7,6},{9,8},{10,9},{11,10},{12... | collective-permute-start | bytes 245768 | tf_op jit(solution)/shard_map/ppermute | solution.py:28
  15.5 12.4 %collective-permute-start.1 = (f32[5,2,32,128]{3,2,1,0:T(8,128)S(1)}, f32[5,2,32,128]{3,2,1,0:T(8,128)S(1)}, u32[]{:S(2)}, u32[]{:S(2)}) collective-permute-start(f32[5,2,32,128]{3,2,1,0:T(8,128)S(1)} %get-tuple-element.41), channel_id=1, source_target_pairs={{8,0},{16,8},{24,16},{32,24},{40,32},{48,40},{56,48},{64,56},{72,6... | collective-permute-start | bytes 491528 | tf_op jit(solution)/shard_map/ppermute | solution.py:28
  18.3 7.7 %collective-permute-start = (f32[5,2,32,128]{3,2,1,0:T(8,128)S(1)}, f32[5,2,32,128]{3,2,1,0:T(8,128)S(1)}, u32[]{:S(2)}, u32[]{:S(2)}) collective-permute-start(f32[5,2,32,128]{3,2,1,0:T(8,128)S(1)} %get-tuple-element.42), channel_id=1, source_target_pairs={{0,8},{8,16},{16,24},{24,32},{32,40},{40,48},{48,56},{56,64},{64,7... | collective-permute-start | bytes 491528 | tf_op jit(solution)/shard_map/ppermute | solution.py:27
  33.7 16.1 %copy-start.13 = (s32[64,1]{0,1:T(1,128)S(1)}, s32[64,1]{0,1:T(1,128)}, u32[]{:S(2)}) copy-start(s32[64,1]{0,1:T(1,128)} %param.10) | copy-start | bytes 772
  38.8 48.7 %collective-permute-start.6 = (f32[5,16,2,128]{3,2,1,0:T(2,128)S(1)}, f32[5,16,2,128]{3,2,1,0:T(2,128)}, u32[]{:S(2)}, u32[]{:S(2)}) collective-permute-start(f32[5,16,2,128]{3,2,1,0:T(2,128)S(1)} %get-tuple-element.34), channel_id=1, source_target_pairs={{0,1},{1,2},{2,3},{3,4},{4,5},{5,6},{6,7},{8,9},{9,10},{10,11},{11... | collective-permute-start | bytes 245768 | tf_op jit(solution)/shard_map/ppermute | solution.py:27
  43.7 44.7 %collective-permute-start.7 = (f32[5,16,2,128]{3,2,1,0:T(2,128)S(1)}, f32[5,16,2,128]{3,2,1,0:T(2,128)}, u32[]{:S(2)}, u32[]{:S(2)}) collective-permute-start(f32[5,16,2,128]{3,2,1,0:T(2,128)S(1)} %get-tuple-element.35), channel_id=1, source_target_pairs={{1,0},{2,1},{3,2},{4,3},{5,4},{6,5},{7,6},{9,8},{10,9},{11,10},{12... | collective-permute-start | bytes 245768 | tf_op jit(solution)/shard_map/ppermute | solution.py:28
  45.0 44.4 %collective-permute-start.4 = (f32[5,2,32,128]{3,2,1,0:T(8,128)S(1)}, f32[5,2,32,128]{3,2,1,0:T(8,128)S(1)}, u32[]{:S(2)}, u32[]{:S(2)}) collective-permute-start(f32[5,2,32,128]{3,2,1,0:T(8,128)S(1)} %get-tuple-element.32), channel_id=1, source_target_pairs={{0,8},{8,16},{16,24},{24,32},{32,40},{40,48},{48,56},{56,64},{64,7... | collective-permute-start | bytes 491528 | tf_op jit(solution)/shard_map/ppermute | solution.py:27
  47.8 41.5 %collective-permute-start.5 = (f32[5,2,32,128]{3,2,1,0:T(8,128)S(1)}, f32[5,2,32,128]{3,2,1,0:T(8,128)S(1)}, u32[]{:S(2)}, u32[]{:S(2)}) collective-permute-start(f32[5,2,32,128]{3,2,1,0:T(8,128)S(1)} %get-tuple-element.33), channel_id=1, source_target_pairs={{8,0},{16,8},{24,16},{32,24},{40,32},{48,40},{56,48},{64,56},{72,6... | collective-permute-start | bytes 491528 | tf_op jit(solution)/shard_map/ppermute | solution.py:28
  102.4 57.4 %collective-permute-start.10 = (f32[5,16,2,128]{3,2,1,0:T(2,128)}, f32[5,16,2,128]{3,2,1,0:T(2,128)}, u32[]{:S(2)}, u32[]{:S(2)}) collective-permute-start(f32[5,16,2,128]{3,2,1,0:T(2,128)} %get-tuple-element.30), channel_id=1, source_target_pairs={{0,1},{1,2},{2,3},{3,4},{4,5},{5,6},{6,7},{8,9},{9,10},{10,11},{11... | collective-permute-start | bytes 245768 | tf_op jit(solution)/shard_map/ppermute | solution.py:27
  107.3 53.5 %collective-permute-start.11 = (f32[5,16,2,128]{3,2,1,0:T(2,128)}, f32[5,16,2,128]{3,2,1,0:T(2,128)}, u32[]{:S(2)}, u32[]{:S(2)}) collective-permute-start(f32[5,16,2,128]{3,2,1,0:T(2,128)} %get-tuple-element.31), channel_id=1, source_target_pairs={{1,0},{2,1},{3,2},{4,3},{5,4},{6,5},{7,6},{9,8},{10,9},{11,10},{12... | collective-permute-start | bytes 245768 | tf_op jit(solution)/shard_map/ppermute | solution.py:28
  108.6 53.1 %collective-permute-start.8 = (f32[5,2,32,128]{3,2,1,0:T(8,128)}, f32[5,2,32,128]{3,2,1,0:T(8,128)S(1)}, u32[]{:S(2)}, u32[]{:S(2)}) collective-permute-start(f32[5,2,32,128]{3,2,1,0:T(8,128)} %get-tuple-element.28), channel_id=1, source_target_pairs={{0,8},{8,16},{16,24},{24,32},{32,40},{40,48},{48,56},{56,64},{64,7... | collective-permute-start | bytes 491528 | tf_op jit(solution)/shard_map/ppermute | solution.py:27
  112.5 49.2 %collective-permute-start.9 = (f32[5,2,32,128]{3,2,1,0:T(8,128)}, f32[5,2,32,128]{3,2,1,0:T(8,128)S(1)}, u32[]{:S(2)}, u32[]{:S(2)}) collective-permute-start(f32[5,2,32,128]{3,2,1,0:T(8,128)} %get-tuple-element.29), channel_id=1, source_target_pairs={{8,0},{16,8},{24,16},{32,24},{40,32},{48,40},{56,48},{64,56},{72,6... | collective-permute-start | bytes 491528 | tf_op jit(solution)/shard_map/ppermute | solution.py:28
  209.0 3.2 copy-start.9
  214.0 40.3 %all-to-all-start = ((bf16[128,2,2049]{2,1,0:T(2,128)(2,1)}), bf16[128,2,2049]{2,1,0:T(2,128)(2,1)S(1)}, u32[]{:S(2)}, u32[]{:S(2)}) async-start(bf16[128,2,2049]{2,1,0:T(2,128)(2,1)} %pad_maximum_fusion.8), calls=%async_computation | async-start | bytes 2228224 | tf_op jit(solution)/shard_map/all_to_all | solution.py:43
  257.8 3.1 copy-start.12
  257.8 3.1 copy-start.14
  257.8 3.1 copy-start.15
  262.9 4.4 copy-start.10
  269.5 38.0 %all-to-all-start.1 = ((bf16[128,2,2,512]{3,2,1,0:T(2,128)(2,1)}), bf16[128,2,2,512]{3,2,1,0:T(2,128)(2,1)S(1)}, u32[]{:S(2)}, u32[]{:S(2)}) async-start(bf16[128,2,2,512]{3,2,1,0:T(2,128)(2,1)} %reshape.81), calls=%async_computation.1 | async-start | bytes 1048576 | tf_op jit(solution)/shard_map/all_to_all | solution.py:177
  274.6 195.1 %all-reduce.11.cloned.1.call-start = ((), (), s32[]{:S(2)}) async-start(), calls=%async_computation.2 | async-start | bytes 10485760 | tf_op jit(solution)/shard_map/psum | solution.py:186
  311.7 5.0 %copy-start.8 = (f32[512,2048]{1,0:T(8,128)S(1)}, f32[512,2048]{1,0:T(8,128)}, u32[]{:S(2)}) copy-start(f32[512,2048]{1,0:T(8,128)} %copy-done.7) | copy-start | bytes 12582916
  469.6 5.6 %copy-start.1 = (bf16[2560,512]{1,0:T(8,128)(2,1)S(1)}, bf16[2560,512]{1,0:T(8,128)(2,1)}, u32[]{:S(2)}) copy-start(bf16[2560,512]{1,0:T(8,128)(2,1)} %param.9) | copy-start | bytes 7864324
  (8 other events, 12.6 us)
Sparse Core Ops, SparseCore 0:
  311.8 157.7 all-reduce.10
where the time goes:
time: 491 us; the launch traced here: 482 us
  waiting for transfers between devices  169 us (34%)
  local copies, waits for them, and re-layouts  166 us (34%)
  starting transfers between devices  60.9 us (12%)
  other arithmetic  47.8 us (10%)
  matrix products  23.2 us (5%)
  between operations  15.2 us (3%)
    psum x1, waiting for transfers between devices, per_device(): patch_gradient = lax.psum(partial_value, ('gx', 'gy'))  149 us
    reshape x3, local copies, waits for them, and re-layouts, patchify(): state.reshape(FIELDS, width_x // PATCH, PATCH, width_y // PATCH, PATCH, w...  43.3 us
    transpose x3, local copies, waits for them, and re-layouts, patchify(): shaped.transpose(1, 3, 5, 0, 2, 4, 6).reshape(-1, FIELDS * PATCH ** 3)  40 us
    ppermute x6, starting transfers between devices, with_halo(): lax.ppermute(last, axis, up)  24.7 us
    reshape x3, local copies, waits for them, and re-layouts, patchify(): shaped.transpose(1, 3, 5, 0, 2, 4, 6).reshape(-1, FIELDS * PATCH ** 3)  23.7 us
    select_n x2, local copies, waits for them, and re-layouts, per_device(): jnp.where(lag_rows == 1, patchify(states[1].astype(jnp.bfloat16)), picked)  20.7 us
    all_to_all x1, starting transfers between devices, sent_together(): lax.all_to_all(both, axis, split_axis=split_dim, concat_axis=concat_dim,...  20.5 us
    all_to_all x1, waiting for transfers between devices, sent_together(): lax.all_to_all(both, axis, split_axis=split_dim, concat_axis=concat_dim,...  19.8 us
  transfers between devices with their start and end apart: 15, of which 2 were waited for; matrix products, arithmetic and copies ran while one was open for 28% of the time, Pallas kernels for 0%

commit v1 on v0

--- a/solution.py
+++ b/solution.py
@@ -183,7 +183,7 @@
     )
     source_grad = returned.reshape(devices * slot_count, BLOCK_ROWS, EMBED)[block_slot]
     partial_value = contract_rows(picked, source_grad.reshape(patch_count, EMBED))
-    patch_gradient = lax.psum(partial_value, ("gx", "gy"))
+    patch_gradient = lax.psum(lax.psum(partial_value, "gx"), "gy")
     return (
         states[-1],
         patch_gradient,

time: 491 us -> 603 us (1.23)
  waiting for transfers between devices: 169 us -> 281 us
    psum x1 -> x2, waiting for transfers between devices: 149 us -> 261 us  [per_device(): patch_gradient = lax.psum(lax.psum(partial_value, 'gx'), 'gy')]
  transfers between devices with their start and end apart: 15 -> 16, of which waited for: 2 -> 3; matrix products, arithmetic and copies ran while one was open for 28% -> 23% of each run, Pallas kernels for 0% -> 0%
where the time goes in v1:
time: 603 us; the launch traced here: 594 us
  waiting for transfers between devices  281 us (47%)
  local copies, waits for them, and re-layouts  166 us (28%)
  starting transfers between devices  61 us (10%)
  other arithmetic  47.8 us (8%)
  matrix products  23.2 us (4%)
  between operations  15.2 us (3%)
    psum x2, waiting for transfers between devices, per_device(): patch_gradient = lax.psum(lax.psum(partial_value, 'gx'), 'gy')  261 us
    reshape x3, local copies, waits for them, and re-layouts, patchify(): state.reshape(FIELDS, width_x // PATCH, PATCH, width_y // PATCH, PATCH, w...  43.3 us
    transpose x3, local copies, waits for them, and re-layouts, patchify(): shaped.transpose(1, 3, 5, 0, 2, 4, 6).reshape(-1, FIELDS * PATCH ** 3)  40 us
    ppermute x6, starting transfers between devices, with_halo(): lax.ppermute(last, axis, up)  24.7 us
    reshape x3, local copies, waits for them, and re-layouts, patchify(): shaped.transpose(1, 3, 5, 0, 2, 4, 6).reshape(-1, FIELDS * PATCH ** 3)  23.7 us
    select_n x2, local copies, waits for them, and re-layouts, per_device(): jnp.where(lag_rows == 1, patchify(states[1].astype(jnp.bfloat16)), picked)  20.7 us
    all_to_all x1, starting transfers between devices, sent_together(): lax.all_to_all(both, axis, split_axis=split_dim, concat_axis=concat_dim,...  20.5 us
    all_to_all x1, waiting for transfers between devices, sent_together(): lax.all_to_all(both, axis, split_axis=split_dim, concat_axis=concat_dim,...  19.8 us
  transfers between devices with their start and end apart: 16, of which 3 were waited for; matrix products, arithmetic and copies ran while one was open for 23% of the time, Pallas kernels for 0%

profile of v1, /device:TPU:1, one launch (start us, length us, event | category | flops | bytes accessed | tf_op | source)
XLA Modules:
  0.0 594.2 jit_solution(6939274358247210894)
XLA Ops:
  8.5 4.7 collective-permute-start.2
  38.8 4.9 collective-permute-start.6
  51.6 14.5 %reshape.74 = bf16[5,2,8,4,8,16,8]{6,5,4,3,2,1,0:T(8,128)(2,1)} reshape(bf16[5,16,32,128]{3,2,1,0:T(8,128)(2,1)} %get-tuple-element.10) | data formatting | bytes 1310720 | tf_op jit(solution)/shard_map/reshape | solution.py:114
  66.1 13.3 %copy.21 = bf16[2,4,16,5,8,8,8]{2,1,0,6,5,4,3:T(4,128)(2,1)} copy(bf16[2,4,16,5,8,8,8]{6,2,5,1,4,0,3:T(8,128)(2,1)} %bitcast.73) | data formatting | bytes 1310720 | tf_op jit(solution)/shard_map/transpose | solution.py:117
  79.4 8.1 %reshape.76 = bf16[128,2560]{0,1:T(8,128)(2,1)} reshape(bf16[2,4,16,5,8,8,8]{2,1,0,6,5,4,3:T(4,128)(2,1)} %copy.21) | data formatting | bytes 1310720 | tf_op jit(solution)/shard_map/reshape | solution.py:117
  102.4 4.9 collective-permute-start.10
  114.6 14.4 %reshape.73 = bf16[5,2,8,4,8,16,8]{6,5,4,3,2,1,0:T(8,128)(2,1)} reshape(bf16[5,16,32,128]{3,2,1,0:T(8,128)(2,1)} %get-tuple-element.8) | data formatting | bytes 1310720 | tf_op jit(solution)/shard_map/reshape | solution.py:114
  129.1 13.3 %copy.20 = bf16[2,4,16,5,8,8,8]{2,1,0,6,5,4,3:T(4,128)(2,1)} copy(bf16[2,4,16,5,8,8,8]{6,2,5,1,4,0,3:T(8,128)(2,1)} %bitcast.74) | data formatting | bytes 1310720 | tf_op jit(solution)/shard_map/transpose | solution.py:117
  142.4 8.1 %reshape.75 = bf16[128,2560]{0,1:T(8,128)(2,1)} reshape(bf16[2,4,16,5,8,8,8]{2,1,0,6,5,4,3:T(4,128)(2,1)} %copy.20) | data formatting | bytes 1310720 | tf_op jit(solution)/shard_map/reshape | solution.py:117
  153.3 5.4 scatter_fusion
  161.7 4.6 select_maximum_fusion
  173.1 14.4 %reshape.78 = bf16[5,2,8,4,8,16,8]{6,5,4,3,2,1,0:T(8,128)(2,1)} reshape(bf16[5,16,32,128]{3,2,1,0:T(8,128)(2,1)} %get-tuple-element.6) | data formatting | bytes 1310720 | tf_op jit(solution)/shard_map/reshape | solution.py:114
  187.6 13.3 %copy.22 = bf16[2,4,16,5,8,8,8]{2,1,0,6,5,4,3:T(4,128)(2,1)} copy(bf16[2,4,16,5,8,8,8]{6,2,5,1,4,0,3:T(8,128)(2,1)} %bitcast.75) | data formatting | bytes 1310720 | tf_op jit(solution)/shard_map/transpose | solution.py:117
  200.9 7.5 %reshape.79 = bf16[128,2560]{0,1:T(8,128)(2,1)S(1)} reshape(bf16[2,4,16,5,8,8,8]{2,1,0,6,5,4,3:T(4,128)(2,1)} %copy.22) | data formatting | bytes 1310720 | tf_op jit(solution)/shard_map/reshape | solution.py:117
  214.0 20.5 %all-to-all-start = ((bf16[128,2,2049]{2,1,0:T(2,128)(2,1)}), bf16[128,2,2049]{2,1,0:T(2,128)(2,1)S(1)}, u32[]{:S(2)}, u32[]{:S(2)}) async-start(bf16[128,2,2049]{2,1,0:T(2,128)(2,1)} %pad_maximum_fusion.8), calls=%async_computation | async-start | bytes 2228224 | tf_op jit(solution)/shard_map/all_to_all | solution.py:43
  234.5 19.8 %all-to-all-done = bf16[128,2,2049]{2,1,0:T(2,128)(2,1)S(1)} async-done(((bf16[128,2,2049]{2,1,0:T(2,128)(2,1)}), bf16[128,2,2049]{2,1,0:T(2,128)(2,1)S(1)}, u32[]{:S(2)}, u32[]{:S(2)}) %all-to-all-start) | async-done | bytes 1049120 | tf_op jit(solution)/shard_map/all_to_all | solution.py:43
  269.5 5.0 all-to-all-start.1
  274.6 12.3 %broadcast_select_fusion = bf16[2,4,16,5,8,8,8]{6,2,5,1,4,0,3:T(8,128)(2,1)} fusion(pred[2,4,16]{2,1,0:T(4,128)(4,1)S(1)} %broadcast_compare_fusion, bf16[5,2,8,4,8,16,8]{6,5,4,3,2,1,0:T(8,128)(2,1)} %reshape.74, bf16[5,2,8,4,8,16,8]{6,5,4,3,2,1,0:T(8,128)(2,1)} %reshape.73), kind=kLoop, calls=%fused_computation.4 | loop fusion | flops 327680 | bytes 1966208 | tf_op jit(solution)/shard_map/jit(_where)/select_n | solution.py:139
  286.9 13.3 %copy.19 = bf16[2,4,16,5,8,8,8]{2,1,0,6,5,4,3:T(4,128)(2,1)} copy(bf16[2,4,16,5,8,8,8]{6,2,5,1,4,0,3:T(8,128)(2,1)} %broadcast_select_fusion) | data formatting | bytes 1310720 | tf_op jit(solution)/shard_map/jit(_where)/select_n | solution.py:139
  300.2 7.3 %select_n.17 = bf16[128,2560]{0,1:T(8,128)(2,1)S(1)} reshape(bf16[2,4,16,5,8,8,8]{2,1,0,6,5,4,3:T(4,128)(2,1)} %copy.19) | data formatting | bytes 1310720 | tf_op jit(solution)/shard_map/jit(_where)/select_n | solution.py:139
  311.7 140.6 %all-reduce.12.cloned.1.call-done = f32[2560,512]{1,0:T(8,128)} async-done(((f32[2560,512]{1,0:T(8,128)}), f32[2560,512]{1,0:T(8,128)}) %all-reduce.12.cloned.1.call-update) | async-done | bytes 5242896 | tf_op jit(solution)/shard_map/psum | solution.py:186
  452.4 5.0 convolution_bitcast_fusion.1
  460.9 120.5 %all-reduce.14.cloned.1.call-done = f32[2560,512]{1,0:T(8,128)} async-done(((f32[2560,512]{1,0:T(8,128)}), f32[2560,512]{1,0:T(8,128)}) %all-reduce.14.cloned.1.call-update) | async-done | bytes 5242896 | tf_op jit(solution)/shard_map/psum | solution.py:186
  581.4 5.6 copy.45
  (141 shorter events, 97.6 us)
Async XLA Ops:
  7.2 143.3 %copy-start = (bf16[2560,512]{1,0:T(8,128)(2,1)S(1)}, bf16[2560,512]{1,0:T(8,128)(2,1)}, u32[]{:S(2)}) copy-start(bf16[2560,512]{1,0:T(8,128)(2,1)} %param.9) | copy-start | bytes 7864324
  8.5 15.7 %collective-permute-start.2 = (f32[5,16,2,128]{3,2,1,0:T(2,128)S(1)}, f32[5,16,2,128]{3,2,1,0:T(2,128)}, u32[]{:S(2)}, u32[]{:S(2)}) collective-permute-start(f32[5,16,2,128]{3,2,1,0:T(2,128)S(1)} %get-tuple-element.39), channel_id=1, source_target_pairs={{0,1},{1,2},{2,3},{3,4},{4,5},{5,6},{6,7},{8,9},{9,10},{10,11},{11... | collective-permute-start | bytes 245768 | tf_op jit(solution)/shard_map/ppermute | solution.py:27
  13.1 11.9 %collective-permute-start.3 = (f32[5,16,2,128]{3,2,1,0:T(2,128)S(1)}, f32[5,16,2,128]{3,2,1,0:T(2,128)}, u32[]{:S(2)}, u32[]{:S(2)}) collective-permute-start(f32[5,16,2,128]{3,2,1,0:T(2,128)S(1)} %get-tuple-element.40), channel_id=1, source_target_pairs={{1,0},{2,1},{3,2},{4,3},{5,4},{6,5},{7,6},{9,8},{10,9},{11,10},{12... | collective-permute-start | bytes 245768 | tf_op jit(solution)/shard_map/ppermute | solution.py:28
  15.5 12.4 %collective-permute-start.1 = (f32[5,2,32,128]{3,2,1,0:T(8,128)S(1)}, f32[5,2,32,128]{3,2,1,0:T(8,128)S(1)}, u32[]{:S(2)}, u32[]{:S(2)}) collective-permute-start(f32[5,2,32,128]{3,2,1,0:T(8,128)S(1)} %get-tuple-element.41), channel_id=1, source_target_pairs={{8,0},{16,8},{24,16},{32,24},{40,32},{48,40},{56,48},{64,56},{72,6... | collective-permute-start | bytes 491528 | tf_op jit(solution)/shard_map/ppermute | solution.py:28
  18.3 7.7 %collective-permute-start = (f32[5,2,32,128]{3,2,1,0:T(8,128)S(1)}, f32[5,2,32,128]{3,2,1,0:T(8,128)S(1)}, u32[]{:S(2)}, u32[]{:S(2)}) collective-permute-start(f32[5,2,32,128]{3,2,1,0:T(8,128)S(1)} %get-tuple-element.42), channel_id=1, source_target_pairs={{0,8},{8,16},{16,24},{24,32},{32,40},{40,48},{48,56},{56,64},{64,7... | collective-permute-start | bytes 491528 | tf_op jit(solution)/shard_map/ppermute | solution.py:27
  33.7 16.1 %copy-start.13 = (s32[64,1]{0,1:T(1,128)S(1)}, s32[64,1]{0,1:T(1,128)}, u32[]{:S(2)}) copy-start(s32[64,1]{0,1:T(1,128)} %param.10) | copy-start | bytes 772
  38.8 48.7 %collective-permute-start.6 = (f32[5,16,2,128]{3,2,1,0:T(2,128)S(1)}, f32[5,16,2,128]{3,2,1,0:T(2,128)}, u32[]{:S(2)}, u32[]{:S(2)}) collective-permute-start(f32[5,16,2,128]{3,2,1,0:T(2,128)S(1)} %get-tuple-element.34), channel_id=1, source_target_pairs={{0,1},{1,2},{2,3},{3,4},{4,5},{5,6},{6,7},{8,9},{9,10},{10,11},{11... | collective-permute-start | bytes 245768 | tf_op jit(solution)/shard_map/ppermute | solution.py:27
  43.7 44.7 %collective-permute-start.7 = (f32[5,16,2,128]{3,2,1,0:T(2,128)S(1)}, f32[5,16,2,128]{3,2,1,0:T(2,128)}, u32[]{:S(2)}, u32[]{:S(2)}) collective-permute-start(f32[5,16,2,128]{3,2,1,0:T(2,128)S(1)} %get-tuple-element.35), channel_id=1, source_target_pairs={{1,0},{2,1},{3,2},{4,3},{5,4},{6,5},{7,6},{9,8},{10,9},{11,10},{12... | collective-permute-start | bytes 245768 | tf_op jit(solution)/shard_map/ppermute | solution.py:28
  45.0 44.4 %collective-permute-start.4 = (f32[5,2,32,128]{3,2,1,0:T(8,128)S(1)}, f32[5,2,32,128]{3,2,1,0:T(8,128)S(1)}, u32[]{:S(2)}, u32[]{:S(2)}) collective-permute-start(f32[5,2,32,128]{3,2,1,0:T(8,128)S(1)} %get-tuple-element.32), channel_id=1, source_target_pairs={{0,8},{8,16},{16,24},{24,32},{32,40},{40,48},{48,56},{56,64},{64,7... | collective-permute-start | bytes 491528 | tf_op jit(solution)/shard_map/ppermute | solution.py:27
  47.8 41.5 %collective-permute-start.5 = (f32[5,2,32,128]{3,2,1,0:T(8,128)S(1)}, f32[5,2,32,128]{3,2,1,0:T(8,128)S(1)}, u32[]{:S(2)}, u32[]{:S(2)}) collective-permute-start(f32[5,2,32,128]{3,2,1,0:T(8,128)S(1)} %get-tuple-element.33), channel_id=1, source_target_pairs={{8,0},{16,8},{24,16},{32,24},{40,32},{48,40},{56,48},{64,56},{72,6... | collective-permute-start | bytes 491528 | tf_op jit(solution)/shard_map/ppermute | solution.py:28
  102.4 57.4 %collective-permute-start.10 = (f32[5,16,2,128]{3,2,1,0:T(2,128)}, f32[5,16,2,128]{3,2,1,0:T(2,128)}, u32[]{:S(2)}, u32[]{:S(2)}) collective-permute-start(f32[5,16,2,128]{3,2,1,0:T(2,128)} %get-tuple-element.30), channel_id=1, source_target_pairs={{0,1},{1,2},{2,3},{3,4},{4,5},{5,6},{6,7},{8,9},{9,10},{10,11},{11... | collective-permute-start | bytes 245768 | tf_op jit(solution)/shard_map/ppermute | solution.py:27
  107.3 53.5 %collective-permute-start.11 = (f32[5,16,2,128]{3,2,1,0:T(2,128)}, f32[5,16,2,128]{3,2,1,0:T(2,128)}, u32[]{:S(2)}, u32[]{:S(2)}) collective-permute-start(f32[5,16,2,128]{3,2,1,0:T(2,128)} %get-tuple-element.31), channel_id=1, source_target_pairs={{1,0},{2,1},{3,2},{4,3},{5,4},{6,5},{7,6},{9,8},{10,9},{11,10},{12... | collective-permute-start | bytes 245768 | tf_op jit(solution)/shard_map/ppermute | solution.py:28
  108.6 53.1 %collective-permute-start.8 = (f32[5,2,32,128]{3,2,1,0:T(8,128)}, f32[5,2,32,128]{3,2,1,0:T(8,128)S(1)}, u32[]{:S(2)}, u32[]{:S(2)}) collective-permute-start(f32[5,2,32,128]{3,2,1,0:T(8,128)} %get-tuple-element.28), channel_id=1, source_target_pairs={{0,8},{8,16},{16,24},{24,32},{32,40},{40,48},{48,56},{56,64},{64,7... | collective-permute-start | bytes 491528 | tf_op jit(solution)/shard_map/ppermute | solution.py:27
  112.5 49.2 %collective-permute-start.9 = (f32[5,2,32,128]{3,2,1,0:T(8,128)}, f32[5,2,32,128]{3,2,1,0:T(8,128)S(1)}, u32[]{:S(2)}, u32[]{:S(2)}) collective-permute-start(f32[5,2,32,128]{3,2,1,0:T(8,128)} %get-tuple-element.29), channel_id=1, source_target_pairs={{8,0},{16,8},{24,16},{32,24},{40,32},{48,40},{56,48},{64,56},{72,6... | collective-permute-start | bytes 491528 | tf_op jit(solution)/shard_map/ppermute | solution.py:28
  209.0 3.2 copy-start.9
  214.0 40.3 %all-to-all-start = ((bf16[128,2,2049]{2,1,0:T(2,128)(2,1)}), bf16[128,2,2049]{2,1,0:T(2,128)(2,1)S(1)}, u32[]{:S(2)}, u32[]{:S(2)}) async-start(bf16[128,2,2049]{2,1,0:T(2,128)(2,1)} %pad_maximum_fusion.8), calls=%async_computation | async-start | bytes 2228224 | tf_op jit(solution)/shard_map/all_to_all | solution.py:43
  257.8 3.1 copy-start.12
  257.8 3.1 copy-start.14
  262.9 4.4 copy-start.10
  269.5 38.0 %all-to-all-start.1 = ((bf16[128,2,2,512]{3,2,1,0:T(2,128)(2,1)}), bf16[128,2,2,512]{3,2,1,0:T(2,128)(2,1)S(1)}, u32[]{:S(2)}, u32[]{:S(2)}) async-start(bf16[128,2,2,512]{3,2,1,0:T(2,128)(2,1)} %reshape.81), calls=%async_computation.1 | async-start | bytes 1048576 | tf_op jit(solution)/shard_map/all_to_all | solution.py:177
  274.6 177.8 %all-reduce.12.cloned.1.call-start = ((), (), s32[]{:S(2)}) async-start(), calls=%async_computation.2 | async-start | bytes 10485760 | tf_op jit(solution)/shard_map/psum | solution.py:186
  311.7 269.7 %all-reduce.14.cloned.1.call-start = ((), (), s32[]{:S(2)}) async-start(), calls=%async_computation.3 | async-start | bytes 10485760 | tf_op jit(solution)/shard_map/psum | solution.py:186
  452.3 5.0 copy-start.8
  581.4 5.6 copy-start.1
  (9 other events, 15.6 us)
Sparse Core Ops, SparseCore 0:
  311.8 140.4 all-reduce.11
  454.8 126.4 all-reduce.13
